TPU v7x, 32 devices: a whole 2x2x4 slice. The times are simulated.
32 devices in a mesh: fsdp: 4 (over x, core), ctx: 8 (over z, y).
Axes of the slice: x: 2, y: 2, z: 4, core: 2. Of those that a mesh axis runs over, the one named last changes fastest.
Arguments:
- tokens: bfloat16 [4, 2048, 1024], P('fsdp', 'ctx'), may hold values from -6 to 6
- out_grad: bfloat16 [4, 2048, 1024], P('fsdp', 'ctx'), may hold values from -6 to 6
- slot_block: int32 [4, 16], P('fsdp'), may hold values from 0 to 15, as said below
- w_attend: bfloat16 [1024, 3072], P('fsdp'), may hold values from -0.1875 to 0.1875
- w_mixing: bfloat16 [1024, 1024], P('fsdp'), may hold values from -1 to 1
- w_expand: bfloat16 [1024, 4096], P('fsdp'), may hold values from -0.1875 to 0.1875
- w_shrink: bfloat16 [4096, 1024], P('fsdp'), may hold values from -0.09375 to 0.09375
- w_norms: bfloat16 [4, 1024], P(None, 'fsdp'), may hold values from -1.2 to 1.4
- first_attend: float32 [1024, 3072], P('fsdp'), may hold values from -24 to 24
- first_mixing: float32 [1024, 1024], P('fsdp'), may hold values from -24 to 24
- first_expand: float32 [1024, 4096], P('fsdp'), may hold values from -24 to 24
- first_shrink: float32 [4096, 1024], P('fsdp'), may hold values from -24 to 24
- first_norms: float32 [4, 1024], P(None, 'fsdp'), may hold values from -24 to 24
- second_attend: float32 [1024, 3072], P('fsdp'), may hold values from 0.5 to 8
- second_mixing: float32 [1024, 1024], P('fsdp'), may hold values from 0.5 to 8
- second_expand: float32 [1024, 4096], P('fsdp'), may hold values from 0.5 to 8
- second_shrink: float32 [4096, 1024], P('fsdp'), may hold values from 0.5 to 8
- second_norms: float32 [4, 1024], P(None, 'fsdp'), may hold values from 0.5 to 8
Outputs:
- layer_out: bfloat16 [4, 2048, 1024], P('fsdp', 'ctx')
- tokens_grad: float32 [4, 2048, 1024], P('fsdp', 'ctx')
- grad_attend: float32 [1024, 3072], P('fsdp')
- update_attend: float32 [1024, 3072], P('fsdp')
- first_new_attend: float32 [1024, 3072], P('fsdp')
- second_new_attend: float32 [1024, 3072], P('fsdp')
- grad_mixing: float32 [1024, 1024], P('fsdp')
- update_mixing: float32 [1024, 1024], P('fsdp')
- first_new_mixing: float32 [1024, 1024], P('fsdp')
- second_new_mixing: float32 [1024, 1024], P('fsdp')
- grad_expand: float32 [1024, 4096], P('fsdp')
- update_expand: float32 [1024, 4096], P('fsdp')
- first_new_expand: float32 [1024, 4096], P('fsdp')
- second_new_expand: float32 [1024, 4096], P('fsdp')
- grad_shrink: float32 [4096, 1024], P('fsdp')
- update_shrink: float32 [4096, 1024], P('fsdp')
- first_new_shrink: float32 [4096, 1024], P('fsdp')
- second_new_shrink: float32 [4096, 1024], P('fsdp')
- grad_norms: float32 [4, 1024], P(None, 'fsdp')
- update_norms: float32 [4, 1024], P(None, 'fsdp')
- first_new_norms: float32 [4, 1024], P(None, 'fsdp')
- second_new_norms: float32 [4, 1024], P(None, 'fsdp')
Inputs may be any that keep to these rules, and one draw needn't show every extreme that they name: `slot_block`: in each row every block number appears once, and slots 2i and 2i+1 hold two blocks whose numbers add up to 15.
All inputs are finite; a program needn't handle non-finite values.
Results may differ from a plain program's by a relative error of at most 0.025.
Values may be sent and summed in bfloat16 or wider, within the bound.
A program may use at most 256 MiB of HBM per device.

v0:
```python
import math
import jax
import jax.numpy as jnp
from jax import lax
from jax.sharding import PartitionSpec as P

HD = 64
HGROUP = 2
STEP_COUNT = 10
EPS_NORM = 1e-05
NEG = -1e30
BETA_ONE = 0.9
BETA_TWO = 0.999
LEARN = 0.02
DECAY = 0.1
EPS_ADAM = 1e-08
CUBIC = 0.044715
ROOT_TWO_PI = math.sqrt(2.0 / math.pi)


def layer_norm(values, gain, shift):
    center = values - jnp.mean(values, axis=-1, keepdims=True)
    spread = jnp.mean(center * center, axis=-1, keepdims=True)
    return center * lax.rsqrt(spread + EPS_NORM) * gain + shift


def gelu(values):
    cube = values * values * values
    return 0.5 * values * (1.0 + jnp.tanh(ROOT_TWO_PI * (values + CUBIC * cube)))


def positions(slots, block):
    offsets = jnp.arange(block, dtype=jnp.int32)
    placed = slots[:, :, None] * block + offsets[None, None, :]
    return placed.reshape(slots.shape[0], slots.shape[1] * block)


def adam_step(weight, grad, first, second):
    first_new = BETA_ONE * first + (1.0 - BETA_ONE) * grad
    second_new = BETA_TWO * second + (1.0 - BETA_TWO) * grad * grad
    mean_hat = first_new / (1.0 - BETA_ONE**STEP_COUNT)
    square_hat = second_new / (1.0 - BETA_TWO**STEP_COUNT)
    update = -LEARN * (
        mean_hat / (jnp.sqrt(square_hat) + EPS_ADAM) + DECAY * weight.astype(jnp.float32)
    )
    return (update, first_new, second_new)


def shards(
    tokens,
    out_grad,
    slot_block,
    w_attend,
    w_mixing,
    w_expand,
    w_shrink,
    w_norms,
    first_attend,
    first_mixing,
    first_expand,
    first_shrink,
    first_norms,
    second_attend,
    second_mixing,
    second_expand,
    second_shrink,
    second_norms,
):
    whole_attend, whole_mixing, whole_expand, whole_shrink, whole_norms = (
        lax.all_gather(w_attend, "fsdp", axis=0, tiled=True),
        lax.all_gather(w_mixing, "fsdp", axis=0, tiled=True),
        lax.all_gather(w_expand, "fsdp", axis=0, tiled=True),
        lax.all_gather(w_shrink, "fsdp", axis=0, tiled=True),
        lax.all_gather(w_norms, "fsdp", axis=1, tiled=True),
    )
    seqs, local, width = tokens.shape
    block = local // 2
    length = slot_block.shape[1] * block
    total_rows = seqs * local
    heads = width // HD
    group_width = HGROUP * HD
    scale = 1.0 / math.sqrt(HD)
    norm_values = whole_norms.astype(jnp.float32)
    owned = lax.dynamic_slice_in_dim(slot_block, 2 * lax.axis_index("ctx"), 2, 1)
    query_place = positions(owned, block)
    key_place = positions(slot_block, block)
    allowed = key_place[:, None, None, :] <= query_place[:, None, :, None]
    start = tokens.reshape(total_rows, width).astype(jnp.float32)
    normed, norm_back = jax.vjp(layer_norm, start, norm_values[0], norm_values[1])
    normed_low = normed.astype(jnp.bfloat16)
    joint = jnp.dot(normed_low, whole_attend, preferred_element_type=jnp.float32).astype(
        jnp.bfloat16
    )
    query = joint[:, :width].reshape(seqs, local, width)
    keys_own = joint[:, width : 2 * width].reshape(seqs, local, width)
    values_own = joint[:, 2 * width :].reshape(seqs, local, width)
    keys, values = (
        lax.all_gather(keys_own, "ctx", axis=1, tiled=True),
        lax.all_gather(values_own, "ctx", axis=1, tiled=True),
    )

    def group_scores(index):
        offset = index * group_width
        query_group = lax.dynamic_slice_in_dim(query, offset, group_width, 2).reshape(
            seqs, local, HGROUP, HD
        )
        key_group = lax.dynamic_slice_in_dim(keys, offset, group_width, 2).reshape(
            seqs, length, HGROUP, HD
        )
        value_group = lax.dynamic_slice_in_dim(values, offset, group_width, 2).reshape(
            seqs, length, HGROUP, HD
        )
        raw = (
            jnp.einsum(
                "sqhd,skhd->shqk", query_group, key_group, preferred_element_type=jnp.float32
            )
            * scale
        )
        return (jnp.where(allowed, raw, NEG), query_group, key_group, value_group)

    def forward_group(index, state):
        mixed_buffer, totals_buffer = state
        masked, query_group, key_group, value_group = group_scores(index)
        top = jnp.max(masked, axis=-1, keepdims=True)
        total = top + jnp.log(jnp.sum(jnp.exp(masked - top), axis=-1, keepdims=True))
        probs = jnp.exp(masked - total).astype(jnp.bfloat16)
        result = jnp.einsum(
            "shqk,skhd->sqhd", probs, value_group, preferred_element_type=jnp.float32
        )
        result = result.reshape(seqs, local, group_width).astype(jnp.bfloat16)
        mixed_buffer = lax.dynamic_update_slice_in_dim(mixed_buffer, result, index * group_width, 2)
        totals_buffer = lax.dynamic_update_slice_in_dim(
            totals_buffer, total[..., 0], index * HGROUP, 1
        )
        return (mixed_buffer, totals_buffer)

    mixed, totals = lax.fori_loop(
        0,
        heads // HGROUP,
        forward_group,
        (
            jnp.zeros((seqs, local, width), jnp.bfloat16),
            jnp.zeros((seqs, heads, local), jnp.float32),
        ),
    )
    mixed_rows = mixed.reshape(total_rows, width)
    middle = start + jnp.dot(mixed_rows, whole_mixing, preferred_element_type=jnp.float32)
    normed_two, norm_two_back = jax.vjp(layer_norm, middle, norm_values[2], norm_values[3])
    normed_two_low = normed_two.astype(jnp.bfloat16)
    expanded = jnp.dot(normed_two_low, whole_expand, preferred_element_type=jnp.float32)
    activated, gelu_back = jax.vjp(gelu, expanded)
    activated_low = activated.astype(jnp.bfloat16)
    result_rows = middle + jnp.dot(activated_low, whole_shrink, preferred_element_type=jnp.float32)
    layer_out = result_rows.reshape(seqs, local, width).astype(jnp.bfloat16)
    incoming = out_grad.reshape(total_rows, width)
    grad_shrink = jnp.dot(activated_low.T, incoming, preferred_element_type=jnp.float32)
    grad_activated = jnp.dot(incoming, whole_shrink.T, preferred_element_type=jnp.float32).astype(
        jnp.bfloat16
    )
    grad_expanded = gelu_back(grad_activated.astype(jnp.float32))[0].astype(jnp.bfloat16)
    grad_expand = jnp.dot(normed_two_low.T, grad_expanded, preferred_element_type=jnp.float32)
    grad_normed_two = jnp.dot(grad_expanded, whole_expand.T, preferred_element_type=jnp.float32)
    grad_middle_norm, grad_gain_two, grad_shift_two = norm_two_back(grad_normed_two)
    grad_middle = incoming.astype(jnp.float32) + grad_middle_norm
    grad_branch = grad_middle.astype(jnp.bfloat16)
    grad_mixing = jnp.dot(mixed_rows.T, grad_branch, preferred_element_type=jnp.float32)
    grad_mixed = jnp.dot(grad_branch, whole_mixing.T, preferred_element_type=jnp.float32)
    grad_mixed = grad_mixed.astype(jnp.bfloat16).reshape(seqs, local, width)

    def backward_group(index, state):
        grad_query, grad_keys, grad_values = state
        offset = index * group_width
        masked, query_group, key_group, value_group = group_scores(index)
        total = lax.dynamic_slice_in_dim(totals, index * HGROUP, HGROUP, 1)
        probs = jnp.exp(masked - total[..., None])
        grad_group = lax.dynamic_slice_in_dim(grad_mixed, offset, group_width, 2).reshape(
            seqs, local, HGROUP, HD
        )
        grad_probs = jnp.einsum(
            "sqhd,skhd->shqk", grad_group, value_group, preferred_element_type=jnp.float32
        )
        grad_scores = probs * (grad_probs - jnp.sum(probs * grad_probs, axis=-1, keepdims=True))
        grad_scores = grad_scores.astype(jnp.bfloat16)
        part_query = (
            jnp.einsum(
                "shqk,skhd->sqhd", grad_scores, key_group, preferred_element_type=jnp.float32
            )
            * scale
        )
        part_keys = (
            jnp.einsum(
                "shqk,sqhd->skhd", grad_scores, query_group, preferred_element_type=jnp.float32
            )
            * scale
        )
        part_values = jnp.einsum(
            "shqk,sqhd->skhd",
            probs.astype(jnp.bfloat16),
            grad_group,
            preferred_element_type=jnp.float32,
        )
        grad_query = lax.dynamic_update_slice_in_dim(
            grad_query, part_query.reshape(seqs, local, group_width), offset, 2
        )
        grad_keys = lax.dynamic_update_slice_in_dim(
            grad_keys, part_keys.reshape(seqs, length, group_width), offset, 2
        )
        grad_values = lax.dynamic_update_slice_in_dim(
            grad_values, part_values.reshape(seqs, length, group_width), offset, 2
        )
        return (grad_query, grad_keys, grad_values)

    grad_query, grad_keys_all, grad_values_all = lax.fori_loop(
        0,
        heads // HGROUP,
        backward_group,
        (
            jnp.zeros((seqs, local, width), jnp.float32),
            jnp.zeros((seqs, length, width), jnp.float32),
            jnp.zeros((seqs, length, width), jnp.float32),
        ),
    )
    grad_keys, grad_values = (
        lax.psum_scatter(
            grad_keys_all.astype(jnp.bfloat16), "ctx", scatter_dimension=1, tiled=True
        ).astype(jnp.float32),
        lax.psum_scatter(
            grad_values_all.astype(jnp.bfloat16), "ctx", scatter_dimension=1, tiled=True
        ).astype(jnp.float32),
    )
    grad_joint = jnp.concatenate(
        [
            grad_query.astype(jnp.bfloat16),
            grad_keys.astype(jnp.bfloat16),
            grad_values.astype(jnp.bfloat16),
        ],
        axis=2,
    ).reshape(total_rows, 3 * width)
    grad_attend = jnp.dot(normed_low.T, grad_joint, preferred_element_type=jnp.float32)
    grad_normed = jnp.dot(grad_joint, whole_attend.T, preferred_element_type=jnp.float32)
    grad_start_norm, grad_gain_one, grad_shift_one = norm_back(grad_normed)
    tokens_grad = (grad_middle + grad_start_norm).reshape(seqs, local, width)
    grad_norms = jnp.stack([grad_gain_one, grad_shift_one, grad_gain_two, grad_shift_two])
    owned_attend, owned_mixing, owned_expand, owned_shrink, owned_norms = (
        lax.psum_scatter(
            grad_attend.astype(jnp.bfloat16), "fsdp", scatter_dimension=0, tiled=True
        ).astype(jnp.float32),
        lax.psum_scatter(
            grad_mixing.astype(jnp.bfloat16), "fsdp", scatter_dimension=0, tiled=True
        ).astype(jnp.float32),
        lax.psum_scatter(
            grad_expand.astype(jnp.bfloat16), "fsdp", scatter_dimension=0, tiled=True
        ).astype(jnp.float32),
        lax.psum_scatter(
            grad_shrink.astype(jnp.bfloat16), "fsdp", scatter_dimension=0, tiled=True
        ).astype(jnp.float32),
        lax.psum_scatter(
            grad_norms.astype(jnp.bfloat16), "fsdp", scatter_dimension=1, tiled=True
        ).astype(jnp.float32),
    )
    sum_attend, sum_mixing, sum_expand, sum_shrink, sum_norms = (
        lax.psum(owned_attend.astype(jnp.bfloat16), "ctx").astype(jnp.float32),
        lax.psum(owned_mixing.astype(jnp.bfloat16), "ctx").astype(jnp.float32),
        lax.psum(owned_expand.astype(jnp.bfloat16), "ctx").astype(jnp.float32),
        lax.psum(owned_shrink.astype(jnp.bfloat16), "ctx").astype(jnp.float32),
        lax.psum(owned_norms.astype(jnp.bfloat16), "ctx").astype(jnp.float32),
    )
    update_attend, first_new_attend, second_new_attend = adam_step(
        w_attend, sum_attend, first_attend, second_attend
    )
    update_mixing, first_new_mixing, second_new_mixing = adam_step(
        w_mixing, sum_mixing, first_mixing, second_mixing
    )
    update_expand, first_new_expand, second_new_expand = adam_step(
        w_expand, sum_expand, first_expand, second_expand
    )
    update_shrink, first_new_shrink, second_new_shrink = adam_step(
        w_shrink, sum_shrink, first_shrink, second_shrink
    )
    update_norms, first_new_norms, second_new_norms = adam_step(
        w_norms, sum_norms, first_norms, second_norms
    )
    return (
        layer_out,
        tokens_grad,
        sum_attend,
        update_attend,
        first_new_attend,
        second_new_attend,
        sum_mixing,
        update_mixing,
        first_new_mixing,
        second_new_mixing,
        sum_expand,
        update_expand,
        first_new_expand,
        second_new_expand,
        sum_shrink,
        update_shrink,
        first_new_shrink,
        second_new_shrink,
        sum_norms,
        update_norms,
        first_new_norms,
        second_new_norms,
    )


def solution(mesh):
    return jax.shard_map(
        shards,
        mesh=mesh,
        in_specs=(
            P("fsdp", "ctx", None),
            P("fsdp", "ctx", None),
            P("fsdp", None),
            P("fsdp", None),
            P("fsdp", None),
            P("fsdp", None),
            P("fsdp", None),
            P(None, "fsdp"),
            P("fsdp", None),
            P("fsdp", None),
            P("fsdp", None),
            P("fsdp", None),
            P(None, "fsdp"),
            P("fsdp", None),
            P("fsdp", None),
            P("fsdp", None),
            P("fsdp", None),
            P(None, "fsdp"),
        ),
        out_specs=(
            P("fsdp", "ctx", None),
            P("fsdp", "ctx", None),
            P("fsdp", None),
            P("fsdp", None),
            P("fsdp", None),
            P("fsdp", None),
            P("fsdp", None),
            P("fsdp", None),
            P("fsdp", None),
            P("fsdp", None),
            P("fsdp", None),
            P("fsdp", None),
            P("fsdp", None),
            P("fsdp", None),
            P("fsdp", None),
            P("fsdp", None),
            P("fsdp", None),
            P("fsdp", None),
            P(None, "fsdp"),
            P(None, "fsdp"),
            P(None, "fsdp"),
            P(None, "fsdp"),
        ),
        check_vma=False,
    )
```

profile of v0, /device:TPU:0, one launch (start us, length us, event | category | flops | bytes accessed | tf_op | source)
XLA Modules:
  0.0 1199.6 jit_solution(6608566212357250092)
XLA Ops:
  8.0 6.3 all_gather.21
  16.8 41.9 %all-gather.9.cloned.1.call-done = bf16[1024,3072]{1,0:T(8,128)(2,1)} async-done(((bf16[256,3072]{1,0:T(8,128)(2,1)}), bf16[1024,3072]{1,0:T(8,128)(2,1)}) %all-gather.9.cloned.1.call-update) | async-done | bytes 6291472 | tf_op jit(solution)/shard_map/all_gather | solution.py:70
  58.7 4.9 convolution_convert_fusion.4
  67.8 70.6 %all-gather.17.cloned.1.call-done = bf16[2048,1024]{1,0:T(8,128)(2,1)} async-done(((bf16[256,1024]{1,0:T(8,128)(2,1)}), bf16[2048,1024]{1,0:T(8,128)(2,1)}) %all-gather.17.cloned.1.call-update) | async-done | bytes 4194320 | tf_op jit(solution)/shard_map/all_gather | solution.py:99
  138.4 6.4 copy.47
  144.8 68.0 %all-gather.19.cloned.1.call-done = bf16[2048,1024]{1,0:T(8,128)(2,1)} async-done(((bf16[256,1024]{1,0:T(8,128)(2,1)}), bf16[2048,1024]{1,0:T(8,128)(2,1)}) %all-gather.19.cloned.1.call-update) | async-done | bytes 4194320 | tf_op jit(solution)/shard_map/all_gather | solution.py:98
  212.8 6.4 copy.49
  219.3 74.3 %while.34 = (s32[]{:T(128)}, bf16[1,256,1024]{1,2,0:T(8,128)(2,1)S(1)}, f32[1,16,256]{2,1,0:T(8,128)S(1)}, bf16[1,2048,1024]{1,2,0:T(8,128)(2,1)}, bf16[1,256,10...) while((s32[]{:T(128)}, ...), condition=%wide.region_5.6_spmd.clone, body=%wide.region_2.5_spmd.clone.sunk | while | flops 276332032 | bytes 33973524 | solution.py:137
  221.0 3.0 fusion.120
  224.1 3.1 exponential_reduce_fusion.2
  230.2 3.0 fusion.120
  233.2 3.1 exponential_reduce_fusion.2
  239.3 3.0 fusion.120
  242.3 3.6 exponential_reduce_fusion.2
  249.6 3.0 fusion.120
  252.7 3.0 exponential_reduce_fusion.2
  258.8 3.0 fusion.120
  261.8 3.0 exponential_reduce_fusion.2
  267.9 3.0 fusion.120
  270.9 3.1 exponential_reduce_fusion.2
  277.0 3.0 fusion.120
  280.1 3.0 exponential_reduce_fusion.2
  286.2 3.0 fusion.120
  289.2 3.0 exponential_reduce_fusion.2
  297.1 7.9 fusion.64
  305.0 49.5 %all-gather.15.cloned.1.call-done = bf16[4096,1024]{1,0:T(8,128)(2,1)} async-done(((bf16[1024,1024]{1,0:T(8,128)(2,1)}), bf16[4096,1024]{1,0:T(8,128)(2,1)}) %all-gather.15.cloned.1.call-update) | async-done | bytes 8388624 | tf_op jit(solution)/shard_map/all_gather | solution.py:73
  354.6 8.7 fusion.17
  363.3 2.7 multiply_reduce_fusion.1
  370.0 2.5 broadcast.290
  375.0 120.1 %while.35 = (s32[]{:T(128)}, bf16[1,256,1024]{1,2,0:T(8,128)(2,1)}, bf16[1,2048,1024]{1,2,0:T(8,128)(2,1)}, bf16[1,2048,1024]{1,2,0:T(8,128)(2,1)}, bf16[1,2048,...) while((s32[]{:T(128)}, bf16[1,256,1024]{1,2,0:T(8,128)(2,1)}, ...), condition=%wide.region_12.13_spmd.clone, body=%wide.region_10.0_spmd.clone.sunk | while | flops 681639424 | bytes 56970552 | solution.py:213
  378.2 2.8 fusion.132
  382.1 4.0 multiply_reduce_fusion.5
  393.2 2.8 fusion.132
  397.2 4.0 multiply_reduce_fusion.5
  408.2 2.8 fusion.132
  412.2 4.0 multiply_reduce_fusion.5
  423.2 2.8 fusion.132
  427.2 4.0 multiply_reduce_fusion.5
  438.2 2.8 fusion.132
  442.2 4.0 multiply_reduce_fusion.5
  453.2 2.8 fusion.132
  457.2 4.0 multiply_reduce_fusion.5
  468.2 2.8 fusion.132
  472.2 4.0 multiply_reduce_fusion.5
  483.3 2.8 fusion.132
  487.2 4.0 multiply_reduce_fusion.5
  496.2 3.1 convolution_convert_fusion.5
  499.5 7.3 convolution_convert_fusion.1
  507.9 8.5 convolution_convert_fusion
  516.4 67.2 %reduce-scatter.12.cloned.1.call-done = bf16[1,256,1024]{1,2,0:T(8,128)(2,1)} async-done(((bf16[1,2048,1024]{1,2,0:T(8,128)(2,1)}), bf16[1,256,1024]{1,2,0:T(8,128)(2,1)}) %reduce-scatter.12.cloned.1.call-update) | async-done | bytes 524304 | tf_op jit(solution)/shard_map/reduce_scatter | solution.py:227
  583.6 92.7 %reduce-scatter.10.cloned.1.call-done = bf16[1,256,1024]{1,2,0:T(8,128)(2,1)} async-done(((bf16[1,2048,1024]{1,2,0:T(8,128)(2,1)}), bf16[1,256,1024]{1,2,0:T(8,128)(2,1)}) %reduce-scatter.10.cloned.1.call-update) | async-done | bytes 524304 | tf_op jit(solution)/shard_map/reduce_scatter | solution.py:224
  676.4 6.0 convolution_convert_fusion.2
  682.5 5.4 fusion.35
  690.7 20.0 %reduce-scatter.16.cloned.1.call-done = bf16[256,1024]{1,0:T(8,128)(2,1)} async-done(((bf16[1024,1024]{1,0:T(8,128)(2,1)}), bf16[256,1024]{1,0:T(8,128)(2,1)}) %reduce-scatter.16.cloned.1.call-update) | async-done | bytes 524304 | tf_op jit(solution)/shard_map/reduce_scatter | solution.py:248
  710.7 74.4 %reduce-scatter.18.cloned.1.call-done = bf16[256,4096]{1,0:T(8,128)(2,1)} async-done(((bf16[1024,4096]{1,0:T(8,128)(2,1)}), bf16[256,4096]{1,0:T(8,128)(2,1)}) %reduce-scatter.18.cloned.1.call-update) | async-done | bytes 2097168 | tf_op jit(solution)/shard_map/reduce_scatter | solution.py:251
  785.0 74.3 %reduce-scatter.20.cloned.1.call-done = bf16[1024,1024]{1,0:T(8,128)(2,1)} async-done(((bf16[4096,1024]{1,0:T(8,128)(2,1)}), bf16[1024,1024]{1,0:T(8,128)(2,1)}) %reduce-scatter.20.cloned.1.call-update) | async-done | bytes 2097168 | tf_op jit(solution)/shard_map/reduce_scatter | solution.py:254
  859.4 60.9 %reduce-scatter.14.cloned.1.call-done = bf16[256,3072]{1,0:T(8,128)(2,1)} async-done(((bf16[1024,3072]{1,0:T(8,128)(2,1)}), bf16[256,3072]{1,0:T(8,128)(2,1)}) %reduce-scatter.14.cloned.1.call-update) | async-done | bytes 1572880 | tf_op jit(solution)/shard_map/reduce_scatter | solution.py:245
  920.4 8.3 fusion.28
  930.2 13.3 %reduce-scatter.22.cloned.1.call-done = bf16[256,4]{1,0:T(8,128)(2,1)} async-done(((bf16[1024,4]{1,0:T(8,128)(2,1)}), bf16[256,4]{1,0:T(8,128)(2,1)}) %reduce-scatter.22.cloned.1.call-update) | async-done | bytes 2064
  944.4 21.8 %psum.39 = bf16[4,256]{1,0:T(4,128)(2,1)S(1)} all-reduce(bf16[4,256]{1,0:T(4,128)(2,1)S(1)} %copy.55), channel_id=1, replica_groups=mesh['fsdp'=4,'ctx'=8] {'ctx'}, use_global_device_ids=true, to_apply=%region_30.31 | all-reduce | flops 1024 | bytes 4096 | tf_op jit(solution)/shard_map/psum | solution.py:266
  966.8 196.3 %all-reduce.3.cloned.1.call-done = (bf16[256,3072]{1,0:T(8,128)(2,1)}, bf16[256,1024]{1,0:T(8,128)(2,1)}, bf16[256,4096]{1,0:T(8,128)(2,1)}, bf16[1024,1024]{1,0:T(8,128)(2,1)}) async-done(((bf16[256,3072]{1,0:T(8,128)(2,1)}, bf16[256,1024]{1,0:T(8,128)(2,1)}, bf16[256,4096]{1,0:T(8,128)(2,1)}, bf16[1024,1024]{1,0:T(8,128)(2,1)}), (bf16[256,3072]{1,0:T(8,128)(2,1)}, bf16[256,1024]{1,0:T(8,128)(2,1)}, ...) | async-done | bytes 6291472 | tf_op jit(solution)/shard_map/psum | solution.py:262
  1163.2 8.7 add_multiply_fusion.2
  1176.2 9.8 add_multiply_fusion.1
  1186.1 6.8 add_multiply_fusion
  (317 shorter events, 119.8 us)
Async XLA Ops:
  7.2 51.5 %all-gather.9.cloned.1.call-start = ((), (), s32[]{:S(2)}) async-start(), calls=%async_computation.7 | async-start | bytes 7864320 | tf_op jit(solution)/shard_map/all_gather | solution.py:70
  7.9 130.4 %all-gather.17.cloned.1.call-start = ((), (), s32[]{:S(2)}) async-start(), calls=%async_computation.17 | async-start | bytes 4718592 | tf_op jit(solution)/shard_map/all_gather | solution.py:99
  16.8 46.8 %copy-start.27 = (f32[256]{0:T(256)}, f32[256]{0:T(256)S(1)}, u32[]{:S(2)}) copy-start(f32[256]{0:T(256)S(1)} %fusion.34) | copy-start | bytes 3076
  63.6 3.7 copy-start.33
  64.7 148.0 %all-gather.19.cloned.1.call-start = ((), (), s32[]{:S(2)}) async-start(), calls=%async_computation.18 | async-start | bytes 4718592 | tf_op jit(solution)/shard_map/all_gather | solution.py:98
  65.5 228.1 %all-gather.11.cloned.1.call-start = ((), (), s32[]{:S(2)}) async-start(), calls=%async_computation.8 | async-start | bytes 2621440 | tf_op jit(solution)/shard_map/all_gather | solution.py:71
  66.1 231.0 %all-gather.13.cloned.1.call-start = ((), (), s32[]{:S(2)}) async-start(), calls=%async_computation.9 | async-start | bytes 10485760 | tf_op jit(solution)/shard_map/all_gather | solution.py:72
  66.6 287.9 %all-gather.15.cloned.1.call-start = ((), (), s32[]{:S(2)}) async-start(), calls=%async_computation.10 | async-start | bytes 10485760 | tf_op jit(solution)/shard_map/all_gather | solution.py:73
  67.2 516.4 %reduce-scatter.12.cloned.1.call-start = ((), (), s32[]{:S(2)}) async-start(), calls=%async_computation.12 | async-start | bytes 4718592 | tf_op jit(solution)/shard_map/reduce_scatter | solution.py:227
  219.2 75.1 %copy-start.2 = (bf16[1,256,1024]{2,1,0:T(8,128)(2,1)S(1)}, bf16[1,256,1024]{2,1,0:T(8,128)(2,1)}, u32[]{:S(2)}) copy-start(bf16[1,256,1024]{2,1,0:T(8,128)(2,1)} %param.22) | copy-start | bytes 1572868
  224.1 3.5 copy-start
  233.2 3.5 copy-start
  242.3 4.7 copy-start
  252.7 3.5 copy-start
  261.8 3.4 copy-start
  270.9 3.5 copy-start
  280.1 3.5 copy-start
  289.2 3.4 copy-start
  293.5 0.8 copy-start.14
  293.6 11.5 copy-start.6
  297.1 57.5 %copy-start.19 = (bf16[1,256,1024]{2,1,0:T(8,128)(2,1)S(1)}, bf16[1,256,1024]{2,1,0:T(8,128)(2,1)}, u32[]{:S(2)}) copy-start(bf16[1,256,1024]{2,1,0:T(8,128)(2,1)} %param.23) | copy-start | bytes 1572868
  354.6 8.7 copy-start.32
  363.3 2.7 copy-start.17
  366.0 1.6 copy-start.18
  367.6 7.4 copy-start.22
  382.1 4.0 copy-start.1
  397.1 4.0 copy-start.1
  412.2 4.0 copy-start.1
  427.2 4.0 copy-start.1
  442.2 4.0 copy-start.1
  457.2 4.0 copy-start.1
  472.2 4.0 copy-start.1
  487.2 4.0 copy-start.1
  495.1 1.0 copy-start.7
  495.2 181.2 %reduce-scatter.10.cloned.1.call-start = ((), (), s32[]{:S(2)}) async-start(), calls=%async_computation.11 | async-start | bytes 4718592 | tf_op jit(solution)/shard_map/reduce_scatter | solution.py:224
  495.9 214.7 %reduce-scatter.16.cloned.1.call-start = ((), (), s32[]{:S(2)}) async-start(), calls=%async_computation.14 | async-start | bytes 2621440 | tf_op jit(solution)/shard_map/reduce_scatter | solution.py:248
  499.3 285.8 %reduce-scatter.18.cloned.1.call-start = ((), (), s32[]{:S(2)}) async-start(), calls=%async_computation.15 | async-start | bytes 10485760 | tf_op jit(solution)/shard_map/reduce_scatter | solution.py:251
  506.8 1.0 copy-start.20
  506.9 352.5 %reduce-scatter.20.cloned.1.call-start = ((), (), s32[]{:S(2)}) async-start(), calls=%async_computation.16 | async-start | bytes 10485760 | tf_op jit(solution)/shard_map/reduce_scatter | solution.py:254
  516.4 160.0 %copy-start.26 = (bf16[1,256,1024]{1,2,0:T(8,128)(2,1)S(1)}, bf16[1,256,1024]{1,2,0:T(8,128)(2,1)}, u32[]{:S(2)}) copy-start(bf16[1,256,1024]{1,2,0:T(8,128)(2,1)} %get-tuple-element.320) | copy-start | bytes 1572868
  516.4 403.9 %reduce-scatter.14.cloned.1.call-start = ((), (), s32[]{:S(2)}) async-start(), calls=%async_computation.13 | async-start | bytes 7864320 | tf_op jit(solution)/shard_map/reduce_scatter | solution.py:245
  682.4 261.1 %reduce-scatter.22.cloned.1.call-start = ((), (), s32[]{:S(2)}) async-start(), calls=%async_computation.19 | async-start | bytes 327680
  682.5 5.5 copy-start.28
  687.9 1.0 copy-start.12
  690.4 472.7 %all-reduce.3.cloned.1.call-start = ((), (), s32[]{:S(2)}) async-start(), calls=%async_computation.20 | async-start | bytes 12582912 | tf_op jit(solution)/shard_map/psum | solution.py:262
  920.3 8.3 copy-start.13
  920.3 8.3 copy-start.21
  928.6 37.6 %copy-start.29 = (bf16[4,256]{1,0:T(4,128)(2,1)S(1)}, bf16[4,256]{1,0:T(4,128)(2,1)}, u32[]{:S(2)}) copy-start(bf16[4,256]{1,0:T(4,128)(2,1)} %param.29) | copy-start | bytes 6148
  928.7 37.6 %copy-start.30 = (f32[4,256]{1,0:T(4,128)S(1)}, f32[4,256]{1,0:T(4,128)}, u32[]{:S(2)}) copy-start(f32[4,256]{1,0:T(4,128)} %param.34) | copy-start | bytes 12292
  928.7 37.6 %copy-start.31 = (f32[4,256]{1,0:T(4,128)S(1)}, f32[4,256]{1,0:T(4,128)}, u32[]{:S(2)}) copy-start(f32[4,256]{1,0:T(4,128)} %param.39) | copy-start | bytes 12292
  928.7 234.5 %copy-start.5 = (bf16[256,3072]{1,0:T(8,128)(2,1)S(1)}, bf16[256,3072]{1,0:T(8,128)(2,1)}, u32[]{:S(2)}) copy-start(bf16[256,3072]{1,0:T(8,128)(2,1)} %param.25) | copy-start | bytes 4718596
  1163.1 8.7 copy-start.16
  1163.1 8.7 copy-start.23
  1163.1 8.7 copy-start.24
  1163.2 8.7 copy-start.25
  1163.2 11.2 copy-start.9
  1171.8 2.5 copy-start.3
  1171.8 4.4 copy-start.8
  1176.2 9.9 copy-start.4
  1176.2 9.9 copy-start.10
  1176.2 9.9 copy-start.11
  1176.2 9.9 copy-start.15
Sparse Core Ops, SparseCore 0:
  9.6 49.0 all-gather.8
  64.9 73.4 all-gather.16
  141.1 71.6 all-gather.18
  214.2 20.8 all-gather.10
  236.5 58.2 all-gather.12
  296.2 58.3 all-gather.14
  495.3 88.2 reduce-scatter.11
  588.3 88.0 reduce-scatter.9
  679.5 31.1 reduce-scatter.15
  713.3 71.7 reduce-scatter.17
  787.6 71.7 reduce-scatter.19
  861.9 58.3 reduce-scatter.13
  923.3 20.0 reduce-scatter.21
  948.4 214.6 all-reduce.2
where the time goes:
time: 1210 us; the launch traced here: 1200 us
  waiting for transfers between devices  833 us (69%)
  matrix products  166 us (14%)
  local copies, waits for them, and re-layouts  87.7 us (7%)
  other arithmetic  68.2 us (6%)
  blocking collectives  28.1 us (2%)
  between operations  14.6 us (1%)
    psum x1, waiting for transfers between devices, shards(): lax.psum(owned_attend.astype(jnp.bfloat16), 'ctx').astype(jnp.float32)  196 us
    reduce_scatter x1, waiting for transfers between devices, shards(): lax.psum_scatter(grad_keys_all.astype(jnp.bfloat16), 'ctx', scatter_dimen...  92.7 us
    reduce_scatter x1, waiting for transfers between devices, shards(): lax.psum_scatter(grad_expand.astype(jnp.bfloat16), 'fsdp', scatter_dimens...  74.4 us
    reduce_scatter x1, waiting for transfers between devices, shards(): lax.psum_scatter(grad_shrink.astype(jnp.bfloat16), 'fsdp', scatter_dimens...  74.3 us
    all_gather x1, waiting for transfers between devices, shards(): lax.all_gather(values_own, 'ctx', axis=1, tiled=True)  70.6 us
    all_gather x1, waiting for transfers between devices, shards(): lax.all_gather(keys_own, 'ctx', axis=1, tiled=True)  68 us
    reduce_scatter x1, waiting for transfers between devices, shards(): lax.psum_scatter(grad_values_all.astype(jnp.bfloat16), 'ctx', scatter_dim...  67.2 us
    reduce_scatter x1, waiting for transfers between devices, shards(): lax.psum_scatter(grad_attend.astype(jnp.bfloat16), 'fsdp', scatter_dimens...  60.9 us
  transfers between devices with their start and end apart: 14, of which 12 were waited for; matrix products, arithmetic and copies ran while one was open for 12% of the time, Pallas kernels for 0%

commit v1 on v0

--- a/solution.py
+++ b/solution.py
@@ -259,7 +259,9 @@
         ).astype(jnp.float32),
     )
     sum_attend, sum_mixing, sum_expand, sum_shrink, sum_norms = (
-        lax.psum(owned_attend.astype(jnp.bfloat16), "ctx").astype(jnp.float32),
+        jnp.sum(lax.all_gather(owned_attend.astype(jnp.bfloat16), "ctx"), axis=0).astype(
+            jnp.float32
+        ),
         lax.psum(owned_mixing.astype(jnp.bfloat16), "ctx").astype(jnp.float32),
         lax.psum(owned_expand.astype(jnp.bfloat16), "ctx").astype(jnp.float32),
         lax.psum(owned_shrink.astype(jnp.bfloat16), "ctx").astype(jnp.float32),

time: 1210 us -> 1330 us (1.099)
  waiting for transfers between devices: 833 us -> 942 us
    all_gather x0 -> x1, waiting for transfers between devices: none -> 154 us  [shards(): lax.all_gather(owned_attend.astype(jnp.bfloat16), 'ctx')]
    psum x1, waiting for transfers between devices: 196 us -> 151 us  [shards(): lax.psum(owned_mixing.astype(jnp.bfloat16), 'ctx').astype(jnp.float32)]
  transfers between devices with their start and end apart: 14 -> 15, of which waited for: 12 -> 13; matrix products, arithmetic and copies ran while one was open for 12% -> 12% of each run, Pallas kernels for 0% -> 0%
where the time goes in v1:
time: 1330 us; the launch traced here: 1320 us
  waiting for transfers between devices  942 us (71%)
  matrix products  166 us (12%)
  local copies, waits for them, and re-layouts  87 us (7%)
  other arithmetic  78.1 us (6%)
  blocking collectives  28.1 us (2%)
  between operations  14.6 us (1%)
    all_gather x1, waiting for transfers between devices, shards(): lax.all_gather(owned_attend.astype(jnp.bfloat16), 'ctx')  154 us
    psum x1, waiting for transfers between devices, shards(): lax.psum(owned_mixing.astype(jnp.bfloat16), 'ctx').astype(jnp.float32)  151 us
    reduce_scatter x1, waiting for transfers between devices, shards(): lax.psum_scatter(grad_keys_all.astype(jnp.bfloat16), 'ctx', scatter_dimen...  92.9 us
    reduce_scatter x1, waiting for transfers between devices, shards(): lax.psum_scatter(grad_expand.astype(jnp.bfloat16), 'fsdp', scatter_dimens...  74.4 us
    reduce_scatter x1, waiting for transfers between devices, shards(): lax.psum_scatter(grad_shrink.astype(jnp.bfloat16), 'fsdp', scatter_dimens...  74.3 us
    all_gather x1, waiting for transfers between devices, shards(): lax.all_gather(values_own, 'ctx', axis=1, tiled=True)  70.6 us
    all_gather x1, waiting for transfers between devices, shards(): lax.all_gather(keys_own, 'ctx', axis=1, tiled=True)  68 us
    reduce_scatter x1, waiting for transfers between devices, shards(): lax.psum_scatter(grad_values_all.astype(jnp.bfloat16), 'ctx', scatter_dim...  67.2 us
  transfers between devices with their start and end apart: 15, of which 13 were waited for; matrix products, arithmetic and copies ran while one was open for 12% of the time, Pallas kernels for 0%

profile of v1, /device:TPU:0, one launch (start us, length us, event | category | flops | bytes accessed | tf_op | source)
XLA Modules:
  0.0 1317.8 jit_solution(3197371802718408301)
XLA Ops:
  8.0 6.3 all_gather.27
  16.8 41.9 %all-gather.11.cloned.1.call-done = bf16[1024,3072]{1,0:T(8,128)(2,1)} async-done(((bf16[256,3072]{1,0:T(8,128)(2,1)}), bf16[1024,3072]{1,0:T(8,128)(2,1)}) %all-gather.11.cloned.1.call-update) | async-done | bytes 6291472 | tf_op jit(solution)/shard_map/all_gather | solution.py:70
  58.7 4.9 convolution_convert_fusion.4
  67.8 70.6 %all-gather.19.cloned.1.call-done = bf16[2048,1024]{1,0:T(8,128)(2,1)} async-done(((bf16[256,1024]{1,0:T(8,128)(2,1)}), bf16[2048,1024]{1,0:T(8,128)(2,1)}) %all-gather.19.cloned.1.call-update) | async-done | bytes 4194320 | tf_op jit(solution)/shard_map/all_gather | solution.py:99
  138.4 6.4 copy.47
  144.8 68.0 %all-gather.21.cloned.1.call-done = bf16[2048,1024]{1,0:T(8,128)(2,1)} async-done(((bf16[256,1024]{1,0:T(8,128)(2,1)}), bf16[2048,1024]{1,0:T(8,128)(2,1)}) %all-gather.21.cloned.1.call-update) | async-done | bytes 4194320 | tf_op jit(solution)/shard_map/all_gather | solution.py:98
  212.8 6.4 copy.49
  219.3 74.3 %while.34 = (s32[]{:T(128)}, bf16[1,256,1024]{1,2,0:T(8,128)(2,1)S(1)}, f32[1,16,256]{2,1,0:T(8,128)S(1)}, bf16[1,2048,1024]{1,2,0:T(8,128)(2,1)}, bf16[1,256,10...) while((s32[]{:T(128)}, ...), condition=%wide.region_5.6_spmd.clone, body=%wide.region_2.5_spmd.clone.sunk | while | flops 276332032 | bytes 33973524 | solution.py:137
  221.0 3.0 fusion.120
  224.1 3.1 exponential_reduce_fusion.2
  230.2 3.0 fusion.120
  233.2 3.1 exponential_reduce_fusion.2
  239.3 3.0 fusion.120
  242.3 3.6 exponential_reduce_fusion.2
  249.6 3.0 fusion.120
  252.7 3.0 exponential_reduce_fusion.2
  258.8 3.0 fusion.120
  261.8 3.0 exponential_reduce_fusion.2
  267.9 3.0 fusion.120
  270.9 3.1 exponential_reduce_fusion.2
  277.0 3.0 fusion.120
  280.1 3.0 exponential_reduce_fusion.2
  286.2 3.0 fusion.120
  289.2 3.0 exponential_reduce_fusion.2
  297.1 7.9 fusion.64
  305.0 49.5 %all-gather.17.cloned.1.call-done = bf16[4096,1024]{1,0:T(8,128)(2,1)} async-done(((bf16[1024,1024]{1,0:T(8,128)(2,1)}), bf16[4096,1024]{1,0:T(8,128)(2,1)}) %all-gather.17.cloned.1.call-update) | async-done | bytes 8388624 | tf_op jit(solution)/shard_map/all_gather | solution.py:73
  354.6 8.7 fusion.17
  375.0 120.1 %while.35 = (s32[]{:T(128)}, bf16[1,256,1024]{1,2,0:T(8,128)(2,1)}, bf16[1,2048,1024]{1,2,0:T(8,128)(2,1)}, bf16[1,2048,1024]{1,2,0:T(8,128)(2,1)}, bf16[1,2048,...) while((s32[]{:T(128)}, bf16[1,256,1024]{1,2,0:T(8,128)(2,1)}, ...), condition=%wide.region_12.13_spmd.clone, body=%wide.region_10.0_spmd.clone.sunk | while | flops 681639424 | bytes 56970552 | solution.py:213
  378.2 2.8 fusion.132
  382.1 4.0 multiply_reduce_fusion.5
  393.2 2.8 fusion.132
  397.2 4.0 multiply_reduce_fusion.5
  408.2 2.8 fusion.132
  412.2 4.0 multiply_reduce_fusion.5
  423.2 2.8 fusion.132
  427.2 4.0 multiply_reduce_fusion.5
  438.2 2.8 fusion.132
  442.2 4.0 multiply_reduce_fusion.5
  453.2 2.8 fusion.132
  457.2 4.0 multiply_reduce_fusion.5
  468.2 2.8 fusion.132
  472.2 4.0 multiply_reduce_fusion.5
  487.2 4.0 multiply_reduce_fusion.5
  496.2 3.1 convolution_convert_fusion.5
  499.5 7.4 convolution_convert_fusion.1
  507.9 8.5 convolution_convert_fusion
  516.5 67.2 %reduce-scatter.12.cloned.1.call-done = bf16[1,256,1024]{1,2,0:T(8,128)(2,1)} async-done(((bf16[1,2048,1024]{1,2,0:T(8,128)(2,1)}), bf16[1,256,1024]{1,2,0:T(8,128)(2,1)}) %reduce-scatter.12.cloned.1.call-update) | async-done | bytes 524304 | tf_op jit(solution)/shard_map/reduce_scatter | solution.py:227
  583.7 92.9 %reduce-scatter.10.cloned.1.call-done = bf16[1,256,1024]{1,2,0:T(8,128)(2,1)} async-done(((bf16[1,2048,1024]{1,2,0:T(8,128)(2,1)}), bf16[1,256,1024]{1,2,0:T(8,128)(2,1)}) %reduce-scatter.10.cloned.1.call-update) | async-done | bytes 524304 | tf_op jit(solution)/shard_map/reduce_scatter | solution.py:224
  676.5 6.1 convolution_convert_fusion.2
  682.8 5.6 fusion.35
  690.9 19.9 %reduce-scatter.16.cloned.1.call-done = bf16[256,1024]{1,0:T(8,128)(2,1)} async-done(((bf16[1024,1024]{1,0:T(8,128)(2,1)}), bf16[256,1024]{1,0:T(8,128)(2,1)}) %reduce-scatter.16.cloned.1.call-update) | async-done | bytes 524304 | tf_op jit(solution)/shard_map/reduce_scatter | solution.py:248
  710.9 74.4 %reduce-scatter.18.cloned.1.call-done = bf16[256,4096]{1,0:T(8,128)(2,1)} async-done(((bf16[1024,4096]{1,0:T(8,128)(2,1)}), bf16[256,4096]{1,0:T(8,128)(2,1)}) %reduce-scatter.18.cloned.1.call-update) | async-done | bytes 2097168 | tf_op jit(solution)/shard_map/reduce_scatter | solution.py:251
  785.2 74.3 %reduce-scatter.20.cloned.1.call-done = bf16[1024,1024]{1,0:T(8,128)(2,1)} async-done(((bf16[4096,1024]{1,0:T(8,128)(2,1)}), bf16[1024,1024]{1,0:T(8,128)(2,1)}) %reduce-scatter.20.cloned.1.call-update) | async-done | bytes 2097168 | tf_op jit(solution)/shard_map/reduce_scatter | solution.py:254
  859.9 60.6 %reduce-scatter.14.cloned.1.call-done = bf16[256,3072]{1,0:T(8,128)(2,1)} async-done(((bf16[1024,3072]{1,0:T(8,128)(2,1)}), bf16[256,3072]{1,0:T(8,128)(2,1)}) %reduce-scatter.14.cloned.1.call-update) | async-done | bytes 1572880 | tf_op jit(solution)/shard_map/reduce_scatter | solution.py:245
  920.5 8.3 fusion.28
  930.3 13.3 %reduce-scatter.22.cloned.1.call-done = bf16[256,4]{1,0:T(8,128)(2,1)} async-done(((bf16[1024,4]{1,0:T(8,128)(2,1)}), bf16[256,4]{1,0:T(8,128)(2,1)}) %reduce-scatter.22.cloned.1.call-update) | async-done | bytes 2064
  944.6 21.9 %psum.31 = bf16[4,256]{1,0:T(4,128)(2,1)S(1)} all-reduce(bf16[4,256]{1,0:T(4,128)(2,1)S(1)} %copy.55), channel_id=1, replica_groups=mesh['fsdp'=4,'ctx'=8] {'ctx'}, use_global_device_ids=true, to_apply=%region_30.31 | all-reduce | flops 1024 | bytes 4096 | tf_op jit(solution)/shard_map/psum | solution.py:268
  967.0 151.5 %all-reduce.3.cloned.1.call-done = (bf16[256,1024]{1,0:T(8,128)(2,1)}, bf16[256,4096]{1,0:T(8,128)(2,1)}, bf16[1024,1024]{1,0:T(8,128)(2,1)}) async-done(((bf16[256,1024]{1,0:T(8,128)(2,1)}, bf16[256,4096]{1,0:T(8,128)(2,1)}, bf16[1024,1024]{1,0:T(8,128)(2,1)}), (bf16[256,1024]{1,0:T(8,128)(2,1)}, bf16[256,4096]{1,0:T(8,128)(2,1)}, bf16[1024,1024]{1,0:T(8,128)(2,1)})) %all-reduce.3.cloned.1.call-update) | async-done | bytes 4718608 | tf_op jit(solution)/shard_map/psum | solution.py:265
  1118.5 4.3 add_multiply_fusion.3
  1122.9 11.3 add_multiply_fusion
  1135.4 7.2 add_multiply_fusion.1
  1142.6 153.6 %all-gather.23.cloned.1.call-done = bf16[2048,3072]{1,0:T(8,128)(2,1)} async-done(((bf16[256,3072]{1,0:T(8,128)(2,1)}), bf16[2048,3072]{1,0:T(8,128)(2,1)}) %all-gather.23.cloned.1.call-update) | async-done | bytes 12582928 | tf_op jit(solution)/shard_map/all_gather | solution.py:262
  1296.2 7.4 reduce_sum.158
  1303.6 7.5 add_multiply_fusion.2
  (307 shorter events, 124.6 us)
Async XLA Ops:
  7.2 51.5 %all-gather.11.cloned.1.call-start = ((), (), s32[]{:S(2)}) async-start(), calls=%async_computation.7 | async-start | bytes 7864320 | tf_op jit(solution)/shard_map/all_gather | solution.py:70
  7.9 130.4 %all-gather.19.cloned.1.call-start = ((), (), s32[]{:S(2)}) async-start(), calls=%async_computation.17 | async-start | bytes 4718592 | tf_op jit(solution)/shard_map/all_gather | solution.py:99
  16.8 46.8 %copy-start.20 = (f32[256]{0:T(256)}, f32[256]{0:T(256)S(1)}, u32[]{:S(2)}) copy-start(f32[256]{0:T(256)S(1)} %fusion.34) | copy-start | bytes 3076
  63.6 3.7 copy-start.26
  64.7 148.0 %all-gather.21.cloned.1.call-start = ((), (), s32[]{:S(2)}) async-start(), calls=%async_computation.18 | async-start | bytes 4718592 | tf_op jit(solution)/shard_map/all_gather | solution.py:98
  65.5 228.1 %all-gather.13.cloned.1.call-start = ((), (), s32[]{:S(2)}) async-start(), calls=%async_computation.8 | async-start | bytes 2621440 | tf_op jit(solution)/shard_map/all_gather | solution.py:71
  66.1 231.0 %all-gather.15.cloned.1.call-start = ((), (), s32[]{:S(2)}) async-start(), calls=%async_computation.9 | async-start | bytes 10485760 | tf_op jit(solution)/shard_map/all_gather | solution.py:72
  66.6 287.9 %all-gather.17.cloned.1.call-start = ((), (), s32[]{:S(2)}) async-start(), calls=%async_computation.10 | async-start | bytes 10485760 | tf_op jit(solution)/shard_map/all_gather | solution.py:73
  67.2 516.4 %reduce-scatter.12.cloned.1.call-start = ((), (), s32[]{:S(2)}) async-start(), calls=%async_computation.12 | async-start | bytes 4718592 | tf_op jit(solution)/shard_map/reduce_scatter | solution.py:227
  219.2 75.1 %copy-start.2 = (bf16[1,256,1024]{2,1,0:T(8,128)(2,1)S(1)}, bf16[1,256,1024]{2,1,0:T(8,128)(2,1)}, u32[]{:S(2)}) copy-start(bf16[1,256,1024]{2,1,0:T(8,128)(2,1)} %param.22) | copy-start | bytes 1572868
  224.1 3.5 copy-start
  233.2 3.5 copy-start
  242.3 4.7 copy-start
  252.7 3.5 copy-start
  261.8 3.4 copy-start
  270.9 3.5 copy-start
  280.1 3.5 copy-start
  289.2 3.4 copy-start
  293.5 0.8 copy-start.13
  293.6 11.5 copy-start.6
  297.1 57.5 %copy-start.17 = (bf16[1,256,1024]{2,1,0:T(8,128)(2,1)S(1)}, bf16[1,256,1024]{2,1,0:T(8,128)(2,1)}, u32[]{:S(2)}) copy-start(bf16[1,256,1024]{2,1,0:T(8,128)(2,1)} %param.23) | copy-start | bytes 1572868
  354.6 8.7 copy-start.25
  363.3 2.7 copy-start.15
  366.0 1.6 copy-start.16
  367.6 7.4 copy-start.19
  382.1 4.0 copy-start.1
  397.1 4.0 copy-start.1
  412.2 4.0 copy-start.1
  427.2 4.0 copy-start.1
  442.2 4.0 copy-start.1
  457.2 4.0 copy-start.1
  472.2 4.0 copy-start.1
  487.2 4.0 copy-start.1
  495.1 1.0 copy-start.7
  495.2 181.4 %reduce-scatter.10.cloned.1.call-start = ((), (), s32[]{:S(2)}) async-start(), calls=%async_computation.11 | async-start | bytes 4718592 | tf_op jit(solution)/shard_map/reduce_scatter | solution.py:224
  495.9 214.9 %reduce-scatter.16.cloned.1.call-start = ((), (), s32[]{:S(2)}) async-start(), calls=%async_computation.14 | async-start | bytes 2621440 | tf_op jit(solution)/shard_map/reduce_scatter | solution.py:248
  499.3 285.9 %reduce-scatter.18.cloned.1.call-start = ((), (), s32[]{:S(2)}) async-start(), calls=%async_computation.15 | async-start | bytes 10485760 | tf_op jit(solution)/shard_map/reduce_scatter | solution.py:251
  506.9 1.0 copy-start.18
  506.9 352.7 %reduce-scatter.20.cloned.1.call-start = ((), (), s32[]{:S(2)}) async-start(), calls=%async_computation.16 | async-start | bytes 10485760 | tf_op jit(solution)/shard_map/reduce_scatter | solution.py:254
  516.4 404.1 %reduce-scatter.14.cloned.1.call-start = ((), (), s32[]{:S(2)}) async-start(), calls=%async_computation.13 | async-start | bytes 7864320 | tf_op jit(solution)/shard_map/reduce_scatter | solution.py:245
  682.7 261.0 %reduce-scatter.22.cloned.1.call-start = ((), (), s32[]{:S(2)}) async-start(), calls=%async_computation.20 | async-start | bytes 327680
  682.8 5.6 copy-start.21
  688.4 1.0 copy-start.11
  690.9 427.6 %all-reduce.3.cloned.1.call-start = ((), (), s32[]{:S(2)}) async-start(), calls=%async_computation.21 | async-start | bytes 9437184 | tf_op jit(solution)/shard_map/psum | solution.py:265
  859.6 436.6 %all-gather.23.cloned.1.call-start = ((), (), s32[]{:S(2)}) async-start(), calls=%async_computation.19 | async-start | bytes 14155776 | tf_op jit(solution)/shard_map/all_gather | solution.py:262
  920.5 8.3 copy-start.12
  928.8 37.6 %copy-start.22 = (bf16[4,256]{1,0:T(4,128)(2,1)S(1)}, bf16[4,256]{1,0:T(4,128)(2,1)}, u32[]{:S(2)}) copy-start(bf16[4,256]{1,0:T(4,128)(2,1)} %param.29) | copy-start | bytes 6148
  928.8 37.6 %copy-start.23 = (f32[4,256]{1,0:T(4,128)S(1)}, f32[4,256]{1,0:T(4,128)}, u32[]{:S(2)}) copy-start(f32[4,256]{1,0:T(4,128)} %param.34) | copy-start | bytes 12292
  928.8 37.6 %copy-start.24 = (f32[4,256]{1,0:T(4,128)S(1)}, f32[4,256]{1,0:T(4,128)}, u32[]{:S(2)}) copy-start(f32[4,256]{1,0:T(4,128)} %param.39) | copy-start | bytes 12292
  930.3 192.6 %copy-start.3 = (bf16[1024,1024]{1,0:T(8,128)(2,1)S(1)}, bf16[1024,1024]{1,0:T(8,128)(2,1)}, u32[]{:S(2)}) copy-start(bf16[1024,1024]{1,0:T(8,128)(2,1)} %param.28) | copy-start | bytes 6291460
  1118.5 4.3 copy-start.8
  1122.9 11.3 copy-start.4
  1122.9 11.3 copy-start.9
  1122.9 11.3 copy-start.10
  1122.9 12.5 copy-start.14
  1296.2 7.4 copy-start.5
Sparse Core Ops, SparseCore 0:
  9.6 49.0 all-gather.10
  64.9 73.4 all-gather.18
  141.1 71.6 all-gather.20
  214.2 20.8 all-gather.12
  236.5 58.2 all-gather.14
  296.2 58.3 all-gather.16
  495.3 88.3 reduce-scatter.11
  588.3 88.2 reduce-scatter.9
  679.7 31.1 reduce-scatter.15
  713.5 71.7 reduce-scatter.17
  787.8 71.7 reduce-scatter.19
  862.1 58.3 reduce-scatter.13
  923.5 20.0 reduce-scatter.21
  948.0 170.4 all-reduce.2
  1120.8 175.3 all-gather.22
